TPU v7x, 512 devices: a whole 4x8x8 slice. The times are simulated.
512 devices in a mesh: occ: 128 (over y, z, core), virt: 4 (over x).
Axes of the slice: x: 4, y: 8, z: 8, core: 2. Of those that a mesh axis runs over, the one named last changes fastest.
Arguments:
- factors: bfloat16 [768, 98304], P('virt', 'occ'), may hold values from -1 to 1
- occ_energy: float32 [64], replicated, may hold values from -2 to -0.5
- virt_energy: float32 [768], replicated, may hold values from 0.2 to 3
- pair_table: int32 [256, 2], P('occ'), may hold values from 0 to 63, as said below
- pair_count: int32 [128], P('occ'), may hold values from 0 to 2, as said below
Outputs:
- gamma: float32 [768, 98304], P('virt', 'occ')
Inputs may be any that keep to these rules, and one draw needn't show every extreme that they name: `pair_table`: each row holds two different orbitals. `pair_count`: the counts sum to exactly 128, and some host has exactly 2.
All inputs are finite; a program needn't handle non-finite values.
Results may differ from a plain program's by a relative error of at most 0.0029.
Values may be sent and summed in bfloat16 or wider, within the bound.
A program may use at most 64 MiB of HBM per device.

v0:
```python
import jax
import jax.numpy as jnp
from jax import lax
from jax.sharding import PartitionSpec as P


def laid_out(blocks, dim):
    dims = list(blocks.shape[1:])
    dims[dim] *= blocks.shape[0]
    return jnp.moveaxis(blocks, 0, dim).reshape(dims)


def gather_together(arrays, axis, dims):
    ravelled = jnp.concatenate([a.reshape(-1) for a in arrays])
    lines, at, finished = (lax.all_gather(ravelled, axis), 0, [])
    for a, dim in zip(arrays, dims):
        blocks = lines[:, at : at + a.size].reshape(-1, *a.shape)
        finished.append(laid_out(blocks, dim))
        at += a.size
    return tuple(finished)


def body(factors, occ_energy, virt_energy, pair_table, pair_count):
    tables, counts = gather_together((pair_table, pair_count), "occ", (0, 0))
    hosts_total = lax.axis_size("occ")
    per_host = pair_table.shape[0]
    entries = jnp.arange(hosts_total * per_host, dtype=jnp.int32)
    active = entries % per_host < jnp.repeat(counts, per_host)
    live_total = per_host * hosts_total // 2
    slot_count = -(-live_total // hosts_total)
    ranking = jnp.cumsum(active.astype(jnp.int32)) - 1
    targets = jnp.arange(hosts_total * slot_count, dtype=jnp.int32)
    select = (active[None, :] & (ranking[None, :] == targets[:, None])).astype(jnp.int32)
    plan = jnp.sum(select[:, :, None] * tables[None, :, :], axis=1).reshape(
        hosts_total, slot_count, 2
    )
    enabled = jnp.max(select, axis=1).reshape(hosts_total, slot_count)
    column = lax.axis_index("virt")
    myself = lax.axis_index("occ")
    orbital_count = occ_energy.shape[0]
    slab_width = factors.shape[0]
    aux_local = factors.shape[1] // orbital_count
    slab_energy = lax.dynamic_slice_in_dim(virt_energy, column * slab_width, slab_width)
    source_cube = factors.reshape(factors.shape[0], aux_local, orbital_count)

    def one_slot(position, accumulated):
        orbitals = lax.dynamic_index_in_dim(plan, position, 1, keepdims=False)
        flags = lax.dynamic_index_in_dim(enabled, position, 1, keepdims=False)
        targets_flat = orbitals.T.reshape(-1)
        picked = jnp.take(source_cube, targets_flat, axis=2)
        outgoing = picked.reshape(factors.shape[0], aux_local, 2, hosts_total)
        incoming = lax.all_to_all(outgoing, "occ", split_axis=3, concat_axis=1, tiled=True)
        both = lax.all_gather(incoming, "virt", axis=0, tiled=True)
        left = both[:, :, 0, 0]
        right = both[:, :, 1, 0]
        mine = lax.dynamic_index_in_dim(orbitals, myself, 0, keepdims=False)
        live_here = lax.dynamic_index_in_dim(flags, myself, 0, keepdims=False).astype(jnp.float32)
        left_slab = lax.dynamic_slice_in_dim(left, column * slab_width, slab_width, 0)
        right_slab = lax.dynamic_slice_in_dim(right, column * slab_width, slab_width, 0)
        couple_rows = lax.dot_general(
            left_slab, right, (((1,), (1,)), ((), ())), preferred_element_type=jnp.float32
        )
        couple_cols = lax.dot_general(
            left, right_slab, (((1,), (1,)), ((), ())), preferred_element_type=jnp.float32
        )
        energy_sum = jnp.take(occ_energy, mine[0]) + jnp.take(occ_energy, mine[1])
        ampl_rows = couple_rows / (energy_sum - slab_energy[:, None] - virt_energy[None, :])
        ampl_cols = couple_cols / (energy_sum - virt_energy[:, None] - slab_energy[None, :])
        mixed_rows = ((2.0 * ampl_rows - ampl_cols.T) * live_here).astype(jnp.bfloat16)
        mixed_cols = ((2.0 * ampl_cols - ampl_rows.T) * live_here).astype(jnp.bfloat16)
        toward_first = jnp.dot(mixed_rows, right, preferred_element_type=jnp.float32)
        toward_second = lax.dot_general(
            mixed_cols, left, (((0,), (0,)), ((), ())), preferred_element_type=jnp.float32
        )
        packed = jnp.stack(
            [toward_first.astype(jnp.bfloat16), toward_second.astype(jnp.bfloat16)], axis=2
        )
        packed = packed.reshape(slab_width, hosts_total, aux_local, 2, 1)
        returned = lax.all_to_all(packed, "occ", split_axis=1, concat_axis=4, tiled=True)
        onehot = (
            targets_flat[:, None] == jnp.arange(orbital_count, dtype=jnp.int32)[None, :]
        ).astype(jnp.bfloat16)
        added = jnp.dot(
            returned.reshape(slab_width * aux_local, 2 * hosts_total),
            onehot,
            preferred_element_type=jnp.float32,
        )
        return accumulated + added.reshape(accumulated.shape)

    start = jnp.zeros(factors.shape, jnp.float32)
    return lax.fori_loop(0, slot_count, one_slot, start)


def solution(mesh):
    in_specs = (P("virt", "occ"), P(), P(), P("occ", None), P("occ"))
    out_specs = P("virt", "occ")
    return jax.shard_map(body, mesh=mesh, in_specs=in_specs, out_specs=out_specs, check_vma=False)
```

profile of v0, /device:TPU:8, one launch (start us, length us, event | category | flops | bytes accessed | tf_op | source)
XLA Modules:
  0.0 244.5 jit_solution(16003386581368237176)
XLA Ops:
  6.5 0.0 all-gather.3.cloned.1.call-start
  6.5 1.1 copy.56
  7.7 0.2 copy.57
  8.5 0.8 reshape.178
  9.3 1.3 dynamic-slice.11
  11.2 0.2 add_dynamic-update-slice_fusion
  11.4 31.4 %all-reduce = s32[640]{0:T(1024)S(1)} all-reduce(s32[640]{0:T(1024)S(1)} %add_dynamic-update-slice_fusion), channel_id=2, replica_groups=mesh['occ'=128,'virt'=4] {'occ'}, use_global_device_ids=true, to_apply=%add | all-reduce | flops 640 | bytes 5120
  42.8 0.2 reshape.254
  43.0 0.2 slice_reduce_fusion
  43.2 0.1 mul.46
  43.3 0.1 copy.55
  43.4 0.1 broadcast_in_dim.47
  43.4 0.1 broadcast_in_dim.48
  43.5 0.2 broadcast_in_dim.49
  43.7 0.3 reduce-window.9
  44.0 0.1 slice.32
  44.1 0.1 slice_reduce_fusion.1
  44.2 0.1 add_bitcast_fusion
  44.3 0.1 broadcast_in_dim.46
  44.4 0.2 reshape.180
  44.6 0.1 multiply_reduce_fusion
  44.8 0.8 gather_fusion
  45.5 2.8 %copy.69 = bf16[192,12,2,128]{3,2,0,1:T(2,128)(2,1)} copy(bf16[192,12,2,128]{0,1,3,2:T(8,128)(2,1)S(1)} %bitcast.73) | data formatting | bytes 2359296 | tf_op jit(solution)/shard_map/while/body/eval_jaxpr/jit(_take)/gather | solution.py:50
  48.3 2.3 broadcast_select_fusion
  50.6 3.2 %copy.59 = bf16[192,12,2,128]{0,2,1,3:T(2,128)(2,1)S(1)} copy(bf16[192,12,2,128]{3,2,0,1:T(2,128)(2,1)S(1)} %broadcast_select_fusion) | data formatting | bytes 2359296 | tf_op jit(solution)/shard_map/while/body/eval_jaxpr/jit(_take)/select_n | solution.py:50
  53.8 48.7 %all_to_all.41 = bf16[192,12,2,128]{0,2,1,3:T(2,128)(2,1)S(1)} all-to-all(bf16[192,12,2,128]{0,2,1,3:T(2,128)(2,1)S(1)} %copy.59), channel_id=1, replica_groups=mesh['occ'=128,'virt'=4] {'occ'}, dimensions={3} | all-to-all | bytes 2359296 | tf_op jit(solution)/shard_map/while/body/eval_jaxpr/all_to_all | solution.py:52
  102.5 0.0 copy-start.1
  102.5 0.0 copy-start
  102.5 4.4 %copy.60 = bf16[192,1536,2,1]{1,2,3,0:T(2,128)(2,1)} copy(bf16[192,1536,2,1]{0,2,1,3:T(2,128)(2,1)S(1)} %bitcast.74) | data formatting | bytes 2359296 | tf_op jit(solution)/shard_map/while/body/eval_jaxpr/all_to_all | solution.py:52
  106.9 0.0 all-gather.3.cloned.1.call-update
  106.9 0.1 constant_dynamic-slice_fusion
  107.0 0.6 fusion.44
  111.6 0.1 fusion.36
  111.7 0.6 dynamic_slice.37
  113.0 0.0 copy-done.1
  113.0 0.6 fusion.45
  114.8 0.0 copy-done
  114.8 0.1 broadcast_subtract_fusion.1
  114.9 43.6 %all-gather.3.cloned.1.call-done = bf16[768,1536,2,1]{1,2,3,0:T(2,128)(2,1)} async-done(((bf16[192,1536,2,1]{1,2,3,0:T(2,128)(2,1)}), bf16[768,1536,2,1]{1,2,3,0:T(2,128)(2,1)}) %all-gather.3.cloned.1.call-update) | async-done | bytes 4718608 | tf_op jit(solution)/shard_map/while/body/eval_jaxpr/all_gather | solution.py:53
  158.5 9.6 %fusion.43 = (bf16[768,1536,1,1]{1,2,3,0:T(2,128)(2,1)S(1)}, bf16[768,1536,1,1]{1,2,3,0:T(2,128)(2,1)S(1)}) fusion(bf16[768,1536,2,1]{1,2,3,0:T(2,128)(2,1)} %all-gather.3.cloned.1.call-done), kind=kLoop, calls=%fused_computation.67 | loop fusion | bytes 9437184 | tf_op jit(solution)/shard_map/while/body/eval_jaxpr/slice | solution.py:55
  168.2 0.6 copy.70
  168.8 0.6 copy.71
  169.4 0.9 fusion.4
  170.3 0.9 fusion.1
  171.2 0.8 convolution_convert_fusion
  172.0 0.8 convolution_convert_fusion.1
  172.8 0.3 copy.64
  173.1 0.2 stack.13
  173.3 0.3 copy.63
  173.6 0.2 stack.12
  173.8 0.4 pad_maximum_fusion
  174.3 2.4 copy.65
  176.7 56.3 %all_to_all.42 = bf16[192,128,12,2,1]{0,3,4,2,1:T(2,128)(2,1)S(1)} all-to-all(bf16[192,128,12,2,1]{0,3,4,2,1:T(2,128)(2,1)S(1)} %copy.65), channel_id=1, replica_groups=mesh['occ'=128,'virt'=4] {'occ'}, dimensions={1} | all-to-all | bytes 2359296 | tf_op jit(solution)/shard_map/while/body/eval_jaxpr/all_to_all | solution.py:79
  233.0 2.9 %copy.66 = bf16[192,1,12,2,128,1]{4,3,2,0,5,1:T(2,128)(2,1)S(1)} copy(bf16[192,1,12,2,128,1]{0,3,2,4,5,1:T(2,128)(2,1)S(1)} %bitcast.75) | data formatting | bytes 2359296 | tf_op jit(solution)/shard_map/while/body/eval_jaxpr/all_to_all | solution.py:79
  236.0 0.5 fusion.6
  236.5 1.1 reshape.186
  (9 shorter events, 0.1 us)
Async XLA Ops:
  6.5 152.0 %all-gather.3.cloned.1.call-start = ((), (), s32[]{:S(2)}) async-start(), calls=%async_computation.2 | async-start | bytes 5898240 | tf_op jit(solution)/shard_map/while/body/eval_jaxpr/all_gather | solution.py:53
  102.5 10.5 %copy-start.1 = (f32[64]{0:T(128)S(1)}, f32[64]{0:T(128)}, u32[]{:S(2)}) copy-start(f32[64]{0:T(128)} %param.6) | copy-start | bytes 772
  102.5 12.3 %copy-start = (f32[768]{0:T(1024)S(1)}, f32[768]{0:T(1024)}, u32[]{:S(2)}) copy-start(f32[768]{0:T(1024)} %param.7) | copy-start | bytes 9220
Sparse Core Ops, SparseCore 0:
  107.0 51.4 all-gather.2
where the time goes:
time: 245 us; the launch traced here: 244 us
  blocking collectives  136 us (56%)
  waiting for transfers between devices  43.6 us (18%)
  local copies, waits for them, and re-layouts  36 us (15%)
  between operations  20.8 us (8%)
  matrix products  3.96 us (2%)
  other arithmetic  3.7 us (2%)
    all_to_all x1, blocking collectives, one_slot(): lax.all_to_all(packed, 'occ', split_axis=1, concat_axis=4, tiled=True)  56.3 us
    all_to_all x1, blocking collectives, one_slot(): lax.all_to_all(outgoing, 'occ', split_axis=3, concat_axis=1, tiled=True)  48.7 us
    all_gather x1, waiting for transfers between devices, one_slot(): both = lax.all_gather(incoming, 'virt', axis=0, tiled=True)  43.6 us
    unnamed x1, blocking collectives  31.4 us
    slice x1, local copies, waits for them, and re-layouts, one_slot(): right = both[:, :, 1, 0]  9.63 us
  transfers between devices with their start and end apart: 1, of which 1 were waited for; matrix products, arithmetic and copies ran while one was open for 1% of the time, Pallas kernels for 0%

commit v1 on v0

--- a/solution.py
+++ b/solution.py
@@ -2,6 +2,11 @@
 import jax.numpy as jnp
 from jax import lax
 from jax.sharding import PartitionSpec as P
+
+
+def swapped_in(x, name, dim):
+    sent = jnp.stack([x] * lax.axis_size(name))
+    return jnp.concatenate(lax.all_to_all(sent, name, 0, 0), axis=dim)
 
 
 def laid_out(blocks, dim):
@@ -50,7 +55,7 @@
         picked = jnp.take(source_cube, targets_flat, axis=2)
         outgoing = picked.reshape(factors.shape[0], aux_local, 2, hosts_total)
         incoming = lax.all_to_all(outgoing, "occ", split_axis=3, concat_axis=1, tiled=True)
-        both = lax.all_gather(incoming, "virt", axis=0, tiled=True)
+        both = swapped_in(incoming, "virt", 0)
         left = both[:, :, 0, 0]
         right = both[:, :, 1, 0]
         mine = lax.dynamic_index_in_dim(orbitals, myself, 0, keepdims=False)

time: 245 us -> 224 us (0.914)
  between operations: 20.8 us -> 7.36 us
  local copies, waits for them, and re-layouts: 36 us -> 27.5 us
  starting transfers between devices: 0.01 us -> 5.24 us
  blocking collectives: 136 us -> 131 us
    all_to_all x0 -> x1, waiting for transfers between devices: none -> 44.7 us  [swapped_in(): return jnp.concatenate(lax.all_to_all(sent, name, 0, 0), axis=dim)]
    all_gather x1 -> x0, waiting for transfers between devices: 43.6 us -> none  [one_slot(): both = lax.all_gather(incoming, 'virt', axis=0, tiled=True)]
    slice x1, local copies, waits for them, and re-layouts: 9.63 us -> 0.31 us  [one_slot(): right = both[:, :, 1, 0]]
    all_to_all x1, blocking collectives: 56.3 us -> 50.5 us  [one_slot(): lax.all_to_all(packed, 'occ', split_axis=1, concat_axis=4, tiled=True)]
    all_to_all x0 -> x1, starting transfers between devices: none -> 5.24 us  [swapped_in(): return jnp.concatenate(lax.all_to_all(sent, name, 0, 0), axis=dim)]
    another operation x2 -> x4, local copies, waits for them, and re-layouts: 0.19 us -> 3.89 us  [the longest x2 3.69 us: swapped_in(): sent = jnp.stack([x] * lax.axis_size(name))]
where the time goes in v1:
time: 224 us; the launch traced here: 223 us
  blocking collectives  131 us (58%)
  waiting for transfers between devices  44.7 us (20%)
  local copies, waits for them, and re-layouts  27.5 us (12%)
  between operations  7.36 us (3%)
  starting transfers between devices  5.24 us (2%)
  matrix products  3.98 us (2%)
  other arithmetic  3.7 us (2%)
    all_to_all x1, blocking collectives, one_slot(): lax.all_to_all(packed, 'occ', split_axis=1, concat_axis=4, tiled=True)  50.5 us
    all_to_all x1, blocking collectives, one_slot(): lax.all_to_all(outgoing, 'occ', split_axis=3, concat_axis=1, tiled=True)  48.7 us
    all_to_all x1, waiting for transfers between devices, swapped_in(): return jnp.concatenate(lax.all_to_all(sent, name, 0, 0), axis=dim)  44.7 us
    unnamed x1, blocking collectives  31.4 us
    all_to_all x1, starting transfers between devices, swapped_in(): return jnp.concatenate(lax.all_to_all(sent, name, 0, 0), axis=dim)  5.24 us
  transfers between devices with their start and end apart: 1, of which 1 were waited for; matrix products, arithmetic and copies ran while one was open for 1% of the time, Pallas kernels for 0%

profile of v1, /device:TPU:8, one launch (start us, length us, event | category | flops | bytes accessed | tf_op | source)
XLA Modules:
  0.0 223.0 jit_solution(14506530048558283184)
XLA Ops:
  0.0 1.1 copy.48
  1.1 0.2 copy.49
  2.0 0.8 reshape.187
  2.8 1.3 dynamic-slice.11
  4.7 0.2 add_dynamic-update-slice_fusion
  4.9 31.4 %all-reduce = s32[640]{0:T(1024)S(1)} all-reduce(s32[640]{0:T(1024)S(1)} %add_dynamic-update-slice_fusion), channel_id=2, replica_groups=mesh['occ'=128,'virt'=4] {'occ'}, use_global_device_ids=true, to_apply=%add | all-reduce | flops 640 | bytes 5120
  36.3 0.2 reshape.264
  36.5 0.2 slice_reduce_fusion
  36.7 0.1 mul.46
  36.8 0.1 copy.47
  36.8 0.1 broadcast_in_dim.47
  36.9 0.1 broadcast_in_dim.48
  37.0 0.2 broadcast_in_dim.49
  37.2 0.3 reduce-window.9
  37.5 0.1 slice.32
  37.6 0.1 slice_reduce_fusion.1
  37.7 0.1 add_bitcast_fusion
  37.8 0.1 broadcast_in_dim.46
  37.9 0.2 reshape.189
  38.1 0.1 multiply_reduce_fusion
  38.2 0.8 gather_fusion
  39.0 2.8 %copy.60 = bf16[192,12,2,128]{3,2,0,1:T(2,128)(2,1)} copy(bf16[192,12,2,128]{0,1,3,2:T(8,128)(2,1)S(1)} %bitcast.79) | data formatting | bytes 2359296 | tf_op jit(solution)/shard_map/while/body/eval_jaxpr/jit(_take)/gather | solution.py:55
  41.8 2.3 %broadcast_select_fusion = bf16[192,12,2,128]{3,2,0,1:T(2,128)(2,1)S(1)} fusion(bf16[192,12,2,128]{3,2,0,1:T(2,128)(2,1)} %copy.60, pred[2,128]{1,0:T(4,128)(4,1)S(1)} %compare_and_fusion), kind=kLoop, calls=%fused_computation.9 | loop fusion | flops 589824 | bytes 2359552 | tf_op jit(solution)/shard_map/while/body/eval_jaxpr/jit(_take)/select_n | solution.py:55
  44.1 3.2 %copy.51 = bf16[192,12,2,128]{0,2,1,3:T(2,128)(2,1)S(1)} copy(bf16[192,12,2,128]{3,2,0,1:T(2,128)(2,1)S(1)} %broadcast_select_fusion) | data formatting | bytes 2359296 | tf_op jit(solution)/shard_map/while/body/eval_jaxpr/jit(_take)/select_n | solution.py:55
  47.3 48.7 %all_to_all.44 = bf16[192,12,2,128]{0,2,1,3:T(2,128)(2,1)S(1)} all-to-all(bf16[192,12,2,128]{0,2,1,3:T(2,128)(2,1)S(1)} %copy.51), channel_id=1, replica_groups=mesh['occ'=128,'virt'=4] {'occ'}, dimensions={3} | all-to-all | bytes 2359296 | tf_op jit(solution)/shard_map/while/body/eval_jaxpr/all_to_all | solution.py:57
  96.0 1.1 copy.52
  97.1 2.6 %stack.24 = bf16[4,192,1536,2,1]{2,1,3,4,0:T(8,128)(2,1)} broadcast(bf16[192,1536,2]{1,0,2:T(8,128)(2,1)S(1)} %copy.52), dimensions={1,2,3} | broadcast | bytes 5898240 | tf_op jit(solution)/shard_map/while/body/eval_jaxpr/stack | solution.py:8
  99.7 0.0 copy-start.1
  99.7 0.0 copy-start
  99.7 5.2 %all-to-all-start.1 = ((bf16[4,192,1536,2,1]{2,1,3,4,0:T(8,128)(2,1)}), bf16[4,192,1536,2,1]{2,1,3,4,0:T(8,128)(2,1)}, u32[]{:S(2)}, u32[]{:S(2)}) async-start(bf16[4,192,1536,2,1]{2,1,3,4,0:T(8,128)(2,1)} %stack.24), calls=%async_computation.1 | async-start | bytes 9437184 | tf_op jit(solution)/shard_map/while/body/eval_jaxpr/all_to_all | solution.py:9
  104.9 0.1 constant_dynamic-slice_fusion
  105.0 0.6 fusion.48
  109.4 0.1 fusion.36
  109.5 0.6 dynamic_slice.37
  110.8 0.0 copy-done.1
  110.8 0.7 fusion.49
  112.8 0.0 copy-done
  112.8 0.1 broadcast_subtract_fusion.1
  112.9 44.7 %all-to-all-done.1 = bf16[4,192,1536,2,1]{2,1,3,4,0:T(8,128)(2,1)} async-done(((bf16[4,192,1536,2,1]{2,1,3,4,0:T(8,128)(2,1)}), bf16[4,192,1536,2,1]{2,1,3,4,0:T(8,128)(2,1)}, u32[]{:S(2)}, u32[]{:S(2)}) %all-to-all-start.1) | async-done | bytes 4718624 | tf_op jit(solution)/shard_map/while/body/eval_jaxpr/all_to_all | solution.py:9
  157.6 2.6 %copy.53 = bf16[4,192,1536,2,1]{2,1,0,3,4:T(8,128)(2,1)S(1)} copy(bf16[4,192,1536,2,1]{2,1,3,4,0:T(8,128)(2,1)} %all-to-all-done.1) | data formatting | bytes 9437184 | tf_op jit(solution)/shard_map/while/body/eval_jaxpr/all_to_all | solution.py:9
  160.2 0.3 fusion.47
  160.5 0.9 fusion.4
  161.5 0.9 fusion.1
  162.4 0.8 convolution_convert_fusion
  163.2 0.8 convolution_convert_fusion.1
  164.0 0.3 copy.55
  164.3 0.2 stack.26
  164.5 0.3 copy.54
  164.8 0.2 stack.25
  165.1 0.4 pad_maximum_fusion
  165.5 2.4 %copy.56 = bf16[192,128,12,2,1]{0,3,4,2,1:T(2,128)(2,1)S(1)} copy(bf16[192,128,12,2,1]{0,2,1,4,3:T(8,128)(2,1)S(1)} %pad_maximum_fusion) | data formatting | bytes 2359296 | tf_op jit(solution)/shard_map/while/body/eval_jaxpr/stack | solution.py:80
  167.9 50.5 %all_to_all.45 = bf16[192,128,12,2,1]{0,3,4,2,1:T(2,128)(2,1)S(1)} all-to-all(bf16[192,128,12,2,1]{0,3,4,2,1:T(2,128)(2,1)S(1)} %copy.56), channel_id=1, replica_groups=mesh['occ'=128,'virt'=4] {'occ'}, dimensions={1} | all-to-all | bytes 2359296 | tf_op jit(solution)/shard_map/while/body/eval_jaxpr/all_to_all | solution.py:84
  218.4 2.9 %copy.57 = bf16[192,1,12,2,128,1]{4,3,2,0,5,1:T(2,128)(2,1)S(1)} copy(bf16[192,1,12,2,128,1]{0,3,2,4,5,1:T(2,128)(2,1)S(1)} %bitcast.81) | data formatting | bytes 2359296 | tf_op jit(solution)/shard_map/while/body/eval_jaxpr/all_to_all | solution.py:84
  221.4 0.5 fusion.6
  221.9 1.1 reshape.196
  (9 shorter events, 0.1 us)
Async XLA Ops:
  99.7 11.1 %copy-start.1 = (f32[64]{0:T(128)S(1)}, f32[64]{0:T(128)}, u32[]{:S(2)}) copy-start(f32[64]{0:T(128)} %param.6) | copy-start | bytes 772
  99.7 13.1 %copy-start = (f32[768]{0:T(1024)S(1)}, f32[768]{0:T(1024)}, u32[]{:S(2)}) copy-start(f32[768]{0:T(1024)} %param.7) | copy-start | bytes 9220
  99.7 57.9 %all-to-all-start.1 = ((bf16[4,192,1536,2,1]{2,1,3,4,0:T(8,128)(2,1)}), bf16[4,192,1536,2,1]{2,1,3,4,0:T(8,128)(2,1)}, u32[]{:S(2)}, u32[]{:S(2)}) async-start(bf16[4,192,1536,2,1]{2,1,3,4,0:T(8,128)(2,1)} %stack.24), calls=%async_computation.1 | async-start | bytes 9437184 | tf_op jit(solution)/shard_map/while/body/eval_jaxpr/all_to_all | solution.py:9
